TPU v7x, 32 devices: a whole 2x2x4 slice. The times are simulated.
32 devices in a mesh: blk: 8 (over z, core), col: 4 (over y, x).
Axes of the slice: x: 2, y: 2, z: 4, core: 2. Of those that a mesh axis runs over, the one named last changes fastest.
Arguments:
- source_coords: bfloat16 [96, 8192], P(None, 'blk'), may hold values from -0.61 to 0.61
- target_coords: bfloat16 [96, 4096], P(None, ('blk', 'col')), may hold values from -0.61 to 0.61
- source_mass: float32 [8192], P('blk'), may hold values from 1.2207031e-05 to 0.0012207031
- target_mass: float32 [4096], P(('blk', 'col')), may hold values from 2.4414063e-05 to 0.0024414062
Outputs:
- source_potential: float32 [8192], P('blk')
- target_potential: float32 [4096], P(('blk', 'col'))
- dual_bound: float32 [], replicated
All inputs are finite; a program needn't handle non-finite values.
Results may differ from a plain program's by a relative error of at most 0.0003.
Values sent between devices are 32-bit elements; how exact they have to be, the bound alone decides.
A program may use at most 64 MiB of HBM per device.

v0:
```python
import math

import jax
import jax.numpy as jnp
from jax import lax
from jax.sharding import PartitionSpec as P

ROUNDS = 2


EPSILON = 0.05
tile_width = 2048


def merged(value, axis, join):
    pieces = jax.tree.map(lambda part: lax.all_gather(part, axis), value)
    head = jax.tree.map(lambda part: part[0], pieces)
    tail = jax.tree.map(lambda part: part[1:], pieces)
    running, _ = lax.scan(lambda running, slab: (join(running, slab), None), head, tail)
    return running


def inner_products(left_coords, right_coords):
    return lax.dot_general(
        left_coords, right_coords, (((0,), (0,)), ((), ())), preferred_element_type=jnp.float32
    )


def split_tiles(values, tile_cols):
    number = values.shape[-1] // tile_cols
    return jnp.moveaxis(values.reshape(values.shape[:-1] + (number, tile_cols)), -2, 0)


def reduce_axis(scores, along):
    maxima = jnp.max(scores, axis=along)
    totals = jnp.sum(jnp.exp(scores - jnp.expand_dims(maxima, along)), axis=along)
    return (maxima, totals)


def merge_lse(first, second):
    first_max, first_sum = first
    second_max, second_sum = second
    maxima = jnp.maximum(first_max, second_max)
    return (
        maxima,
        first_sum * jnp.exp(first_max - maxima) + second_sum * jnp.exp(second_max - maxima),
    )


def squares_of(coords):
    return jnp.sum(jnp.square(coords.astype(jnp.float32)), axis=0)


def cost_tile(left_coords, right_coords, left_sq, right_sq):
    return left_sq[:, None] + right_sq[None, :] - 2.0 * inner_products(left_coords, right_coords)


def gather_duals(col_dual):
    return lax.all_gather(col_dual, "blk", axis=0, tiled=True)


def local(source_coords, target_coords, source_mass, target_mass):
    source_count = source_coords.shape[1]
    target_count = target_coords.shape[1]
    source_sq = squares_of(source_coords)
    source_logs = jnp.log(source_mass)
    target_logs = jnp.log(target_mass)
    held_wide, held_logs = (
        lax.all_gather(target_coords.astype(jnp.float32), "blk", axis=1, tiled=True),
        lax.all_gather(target_logs, "blk", axis=0, tiled=True),
    )
    held_sq = squares_of(held_wide)
    held_coords = held_wide.astype(jnp.bfloat16)
    held_count = held_coords.shape[1]
    tile_cols = math.gcd(held_count, tile_width)
    coord_tiles = split_tiles(held_coords, tile_cols)
    square_tiles = split_tiles(held_sq, tile_cols)
    log_tiles = split_tiles(held_logs, tile_cols)

    def row_pass(held_dual):

        def advance(partial_value, element):
            tile_coords, tile_sq, tile_logs, tile_dual = element
            scores = (
                tile_logs[None, :]
                + (tile_dual[None, :] - cost_tile(source_coords, tile_coords, source_sq, tile_sq))
                / EPSILON
            )
            return (merge_lse(partial_value, reduce_axis(scores, 1)), None)

        blank_rows = (
            jnp.full((source_count,), -jnp.inf, jnp.float32),
            jnp.zeros((source_count,), jnp.float32),
        )
        result, _ = lax.scan(
            advance,
            blank_rows,
            (coord_tiles, square_tiles, log_tiles, split_tiles(held_dual, tile_cols)),
        )
        return result

    col_dual = jnp.zeros((target_count,), jnp.float32)
    held_dual = jnp.zeros((held_count,), jnp.float32)
    for round_index in range(ROUNDS):
        if round_index > 0:
            held_dual = gather_duals(col_dual)
        partial_rows = row_pass(held_dual)
        row_max, row_sum = merged(partial_rows, "col", merge_lse)
        row_dual = -EPSILON * (row_max + jnp.log(row_sum))

        def column_tile(element):
            tile_coords, tile_sq = element
            scores = (
                source_logs[:, None]
                + (row_dual[:, None] - cost_tile(source_coords, tile_coords, source_sq, tile_sq))
                / EPSILON
            )
            return reduce_axis(scores, 0)

        part_max, part_sum = lax.map(column_tile, (coord_tiles, square_tiles))
        whole_max, whole_sum = merged(
            (part_max.reshape(held_count), part_sum.reshape(held_count)), "blk", merge_lse
        )
        start = lax.axis_index("blk") * target_count
        col_max = lax.dynamic_slice_in_dim(whole_max, start, target_count)
        col_sum = lax.dynamic_slice_in_dim(whole_sum, start, target_count)
        col_dual = -EPSILON * (col_max + jnp.log(col_sum))
    held_dual = gather_duals(col_dual)

    def lower(partial_value, element):
        tile_coords, tile_sq, tile_dual = element
        values = cost_tile(source_coords, tile_coords, source_sq, tile_sq) - tile_dual[None, :]
        return (jnp.minimum(partial_value, jnp.min(values, axis=1)), None)

    lowest, _ = lax.scan(
        lower,
        jnp.full((source_count,), jnp.inf, jnp.float32),
        (coord_tiles, square_tiles, split_tiles(held_dual, tile_cols)),
    )
    source_potential = lax.pmin(lowest, "col")
    source_part = jnp.sum(source_mass * source_potential) * (1.0 / lax.axis_size("col"))
    target_part = jnp.sum(target_mass * col_dual)
    source_total, target_total = lax.psum((source_part, target_part), ("blk", "col"))
    return (source_potential, col_dual, source_total + target_total)


def solution(mesh):
    in_specs = (P(None, "blk"), P(None, ("blk", "col")), P("blk"), P(("blk", "col")))
    out_specs = (P("blk"), P(("blk", "col")), P())
    return jax.shard_map(local, mesh=mesh, in_specs=in_specs, out_specs=out_specs, check_vma=False)
```

profile of v0, /device:TPU:0, one launch (start us, length us, event | category | flops | bytes accessed | tf_op | source)
XLA Modules:
  0.0 209.7 jit_solution(9440462821421479608)
XLA Ops:
  1.3 13.5 %all-gather.6 = f32[8,1,128]{2,1,0:T(1,128)S(1)} all-gather(f32[1,1,128]{2,1,0:T(1,128)S(1)} %log_bitcast_fusion), channel_id=1, replica_groups=mesh['blk'=8,'col'=4] {'blk'}, dimensions={0}, use_global_device_ids=true | all-gather | bytes 4608 | tf_op jit(solution)/shard_map/all_gather | solution.py:70
  15.5 14.4 %all_gather.44 = f32[96,1024]{1,0:T(8,128)S(1)} all-gather(f32[96,128]{1,0:T(8,128)S(1)} %convert_element_type.10), channel_id=1, replica_groups=mesh['blk'=8,'col'=4] {'blk'}, dimensions={1}, use_global_device_ids=true | all-gather | bytes 442368 | tf_op jit(solution)/shard_map/all_gather | solution.py:69
  31.0 2.2 %fusion = (f32[1024]{0:T(1024)S(1)}, f32[1024,1024]{0,1:T(8,128)S(1)}) fusion(f32[1024]{0:T(1024)S(1)} %bitcast.55, bf16[96,1024]{1,0:T(8,128)(2,1)} %param.12, f32[96,1024]{1,0:T(8,128)S(1)} %all_gather.44, f32[1024]{0:T(1024)S(1)} %multiply_reduce_fusion, f32[1024]{0:T(1024)S(1)} %multiply_reduce_fusion.1), kind=kOutput, calls=%fused_computation.22 | convolution fusion | flops 208763904 | bytes 4800512 | tf_op jit(solution)/shard_map/while/body/eval_jaxpr/dot_general | solution.py:24
  33.2 1.9 copy-done
  35.1 1.0 exponential_reduce_fusion.3
  36.1 8.2 %all-gather.7 = f32[4,1,1024]{2,1,0:T(1,128)S(1)} all-gather(f32[1,1,1024]{2,1,0:T(1,128)S(1)} %bitcast.61), channel_id=1, replica_groups=mesh['blk'=8,'col'=4] {'col'}, dimensions={0}, use_global_device_ids=true | all-gather | bytes 20480 | tf_op jit(solution)/shard_map/all_gather | solution.py:16
  44.3 8.2 %all-gather = f32[4096]{0:T(1024)S(1)} all-gather(f32[1024]{0:T(1024)S(1)} %get-tuple-element.307), channel_id=2, replica_groups=mesh['blk'=8,'col'=4] {'col'}, dimensions={0}, use_global_device_ids=true | all-gather | bytes 20480 | tf_op jit(solution)/shard_map/all_gather | solution.py:16
  52.7 3.0 %fusion.1 = f32[1024]{0:T(1024)S(1)} fusion(f32[1024,1024]{0,1:T(8,128)} %copy-done, f32[1024]{0:T(1024)S(1)} %add_multiply_fusion.1, f32[1024]{0:T(1024)S(1)} %log.18), kind=kLoop, calls=%fused_computation.23 | loop fusion | flops 4193280 | bytes 4206592 | tf_op jit(solution)/shard_map/while/body/eval_jaxpr/reduce_max | solution.py:35
  56.1 1.1 exponential_reduce_fusion.2
  57.2 14.1 %all-gather.2 = f32[8192]{0:T(1024)S(1)} all-gather(f32[1024]{0:T(1024)S(1)} %exponential_reduce_fusion.2), channel_id=4, replica_groups=mesh['blk'=8,'col'=4] {'blk'}, dimensions={0}, use_global_device_ids=true | all-gather | bytes 36864 | tf_op jit(solution)/shard_map/all_gather | solution.py:16
  71.3 14.1 %all-gather.1 = f32[8192]{0:T(1024)S(1)} all-gather(f32[1024]{0:T(1024)S(1)} %fusion.1), channel_id=3, replica_groups=mesh['blk'=8,'col'=4] {'blk'}, dimensions={0}, use_global_device_ids=true | all-gather | bytes 36864 | tf_op jit(solution)/shard_map/all_gather | solution.py:16
  85.9 8.9 %all-gather.8 = f32[8,1,128]{2,1,0:T(1,128)S(1)} all-gather(f32[1,1,128]{2,1,0:T(1,128)S(1)} %multiply_bitcast_fusion), channel_id=1, replica_groups=mesh['blk'=8,'col'=4] {'blk'}, dimensions={0}, use_global_device_ids=true | all-gather | bytes 4608 | tf_op jit(solution)/shard_map/all_gather | solution.py:59
  94.8 2.8 %fusion.2 = f32[1024]{0:T(1024)S(1)} fusion(f32[1024,1024]{0,1:T(8,128)} %copy-done, f32[1024]{0:T(1024)S(1)} %bitcast.59, f32[1024]{0:T(1024)S(1)} %bitcast.57), kind=kLoop, calls=%fused_computation.24 | loop fusion | flops 4193280 | bytes 4206592 | tf_op jit(solution)/shard_map/while/body/eval_jaxpr/reduce_max | solution.py:35
  97.6 1.0 exponential_reduce_fusion.1
  98.7 7.2 %all-gather.9 = f32[4,1,1024]{2,1,0:T(1,128)S(1)} all-gather(f32[1,1,1024]{2,1,0:T(1,128)S(1)} %bitcast.62), channel_id=1, replica_groups=mesh['blk'=8,'col'=4] {'col'}, dimensions={0}, use_global_device_ids=true | all-gather | bytes 20480 | tf_op jit(solution)/shard_map/all_gather | solution.py:16
  105.9 8.2 %all-gather.3 = f32[4096]{0:T(1024)S(1)} all-gather(f32[1024]{0:T(1024)S(1)} %fusion.2), channel_id=5, replica_groups=mesh['blk'=8,'col'=4] {'col'}, dimensions={0}, use_global_device_ids=true | all-gather | bytes 20480 | tf_op jit(solution)/shard_map/all_gather | solution.py:16
  114.3 3.0 %fusion.3 = f32[1024]{0:T(1024)S(1)} fusion(f32[1024,1024]{0,1:T(8,128)} %copy-done, f32[1024]{0:T(1024)S(1)} %add_multiply_fusion, f32[1024]{0:T(1024)S(1)} %log.18), kind=kLoop, calls=%fused_computation.25 | loop fusion | flops 4193280 | bytes 4206592 | tf_op jit(solution)/shard_map/while/body/eval_jaxpr/reduce_max | solution.py:35
  117.7 1.2 exponential_reduce_fusion
  118.8 14.1 %all-gather.5 = f32[8192]{0:T(1024)S(1)} all-gather(f32[1024]{0:T(1024)S(1)} %exponential_reduce_fusion), channel_id=7, replica_groups=mesh['blk'=8,'col'=4] {'blk'}, dimensions={0}, use_global_device_ids=true | all-gather | bytes 36864 | tf_op jit(solution)/shard_map/all_gather | solution.py:16
  132.9 14.1 %all-gather.4 = f32[8192]{0:T(1024)S(1)} all-gather(f32[1024]{0:T(1024)S(1)} %fusion.3), channel_id=6, replica_groups=mesh['blk'=8,'col'=4] {'blk'}, dimensions={0}, use_global_device_ids=true | all-gather | bytes 36864 | tf_op jit(solution)/shard_map/all_gather | solution.py:16
  148.1 10.0 %all-gather.10 = f32[8,1,128]{2,1,0:T(1,128)S(1)} all-gather(f32[1,1,128]{2,1,0:T(1,128)S(1)} %bitcast.64), channel_id=1, replica_groups=mesh['blk'=8,'col'=4] {'blk'}, dimensions={0}, use_global_device_ids=true | all-gather | bytes 4608 | tf_op jit(solution)/shard_map/all_gather | solution.py:59
  158.1 2.5 %subtract_reduce_fusion = f32[1024]{0:T(1024)S(1)} fusion(f32[1024,1024]{0,1:T(8,128)} %copy-done, f32[1024]{0:T(1024)S(1)} %bitcast.63), kind=kLoop, calls=%fused_computation.12 | loop fusion | flops 2096128 | bytes 4202496 | tf_op jit(solution)/shard_map/while/body/eval_jaxpr/reduce_min | solution.py:133
  160.7 8.9 %pmin.7 = f32[1024]{0:T(1024)S(1)} all-reduce(f32[1024]{0:T(1024)S(1)} %subtract_reduce_fusion), channel_id=1, replica_groups=mesh['blk'=8,'col'=4] {'col'}, use_global_device_ids=true, to_apply=%region_19.20 | all-reduce | flops 1024 | bytes 8192 | tf_op jit(solution)/shard_map/pmin | solution.py:140
  171.6 38.1 %psum.16 = f32[]{:T(128)} all-reduce(f32[]{:T(128)S(6)} %add.217), channel_id=1, replica_groups=mesh['blk'=8,'col'=4] {'blk','col'}, use_global_device_ids=true, to_apply=%region_21.22 | all-reduce | flops 1 | bytes 8 | tf_op jit(solution)/shard_map/psum | solution.py:143
  (95 shorter events, 6.4 us)
Async XLA Ops:
  33.1 1.9 copy-start
  33.2 19.5 %copy-start.4 = (f32[1024]{0:T(1024)S(1)}, f32[1024]{0:T(1024)}, u32[]{:S(2)}) copy-start(f32[1024]{0:T(1024)} %param.14) | copy-start | bytes 12292
  52.6 3.5 %copy-start.1 = (f32[1024,1024]{0,1:T(8,128)S(1)}, f32[1024,1024]{0,1:T(8,128)}, u32[]{:S(2)}) copy-start(f32[1024,1024]{0,1:T(8,128)} %copy-done) | copy-start | bytes 12582916
  85.8 11.8 %copy-start.2 = (f32[1024,1024]{0,1:T(8,128)S(1)}, f32[1024,1024]{0,1:T(8,128)}, u32[]{:S(2)}) copy-start(f32[1024,1024]{0,1:T(8,128)} %copy-done) | copy-start | bytes 12582916
  114.2 3.5 %copy-start.3 = (f32[1024,1024]{0,1:T(8,128)S(1)}, f32[1024,1024]{0,1:T(8,128)}, u32[]{:S(2)}) copy-start(f32[1024,1024]{0,1:T(8,128)} %copy-done) | copy-start | bytes 12582916
  114.3 33.2 %copy-start.7 = (f32[128]{0:T(128)S(1)}, f32[128]{0:T(128)}, u32[]{:S(2)}) copy-start(f32[128]{0:T(128)} %param.15) | copy-start | bytes 1540
  148.1 61.6 %copy-start.6 = (f32[128]{0:T(128)}, f32[128]{0:T(128)S(1)}, u32[]{:S(2)}) copy-start(f32[128]{0:T(128)S(1)} %get-tuple-element.298) | copy-start | bytes 1540
  169.6 40.1 %copy-start.5 = (f32[1024]{0:T(1024)}, f32[1024]{0:T(1024)S(1)}, u32[]{:S(2)}) copy-start(f32[1024]{0:T(1024)S(1)} %pmin.7) | copy-start | bytes 12292
where the time goes:
time: 210 us
  blocking collectives  182 us (87%)
  other arithmetic  19.1 us (9%)
  local copies, waits for them, and re-layouts  3.84 us (2%)
  between operations  2.23 us (1%)
  matrix products  2.19 us (1%)
    all_gather x8, blocking collectives, merged(): pieces = jax.tree.map(lambda part: lax.all_gather(part, axis), value)  88.1 us
    psum x1, blocking collectives, local(): lax.psum((source_part, target_part), ('blk', 'col'))  38.1 us
    all_gather x2, blocking collectives, gather_duals(): return lax.all_gather(col_dual, 'blk', axis=0, tiled=True)  18.9 us
    all_gather x1, blocking collectives, local(): lax.all_gather(target_coords.astype(jnp.float32), 'blk', axis=1, tiled=True)  14.4 us
    all_gather x1, blocking collectives, local(): lax.all_gather(target_logs, 'blk', axis=0, tiled=True)  13.5 us
    pmin x1, blocking collectives, local(): source_potential = lax.pmin(lowest, 'col')  8.94 us
    reduce_max x3, other arithmetic, reduce_axis(): maxima = jnp.max(scores, axis=along)  8.72 us
    reduce_sum x4, other arithmetic, reduce_axis(): jnp.sum(jnp.exp(scores - jnp.expand_dims(maxima, along)), axis=along)  4.32 us

commit v1 on v0

v1 whole, which is shorter than its diff:
```python
import functools

import jax
import jax.numpy as jnp
from jax import lax
from jax.experimental import pallas as pl
from jax.experimental.pallas import tpu as pltpu
from jax.sharding import PartitionSpec as P

ROUNDS = 2
EPSILON = 0.05
LANES = 128
EXTRA = 8
F32 = jnp.float32
BF16 = jnp.bfloat16
SCALE = 1.4426950408889634 / EPSILON
MESH = pl.DeviceIdType.MESH


def soft(total):
    return EPSILON * jnp.log(total)


def row_tile(reds, wide):
    position = lax.broadcasted_iota(jnp.int32, (8, LANES), 0)
    out = jnp.zeros((8, LANES), F32)
    for index, part in enumerate(reds):
        out = jnp.where(position == index, jnp.broadcast_to(part, (8, LANES)), out)
    return out


def three_parts(value):
    high = value.astype(BF16).astype(F32)
    rest = value - high
    middle = rest.astype(BF16).astype(F32)
    return high, middle, rest - middle


def set_bias(left_ref, value, feats_pad):
    parts = three_parts(value)
    for r in range(value.shape[0]):
        tile = row_tile([part[r : r + 1, :] for part in parts], LANES)
        left_ref[r * LANES : (r + 1) * LANES, feats_pad : feats_pad + 8] = tile.T.astype(BF16)


def reduce_pass(left_ref, right_ref, out_ref, slot, hard, chunk):
    number = right_ref.shape[1] // chunk

    def body(c, carry):
        lanes = pl.ds(pl.multiple_of(c * chunk, chunk), chunk)
        scores = jnp.dot(left_ref[...], right_ref[:, lanes], preferred_element_type=F32)
        value = jnp.max(scores, axis=0, keepdims=True)
        if not hard:
            total = jnp.sum(jnp.exp2((scores - value) * SCALE), axis=0, keepdims=True)
            value = value + soft(total)
        for r in range(chunk // LANES):
            out_ref[slot, pl.ds(c * (chunk // LANES) + r, 1), :] = value[
                :, r * LANES : (r + 1) * LANES
            ]
        return carry

    lax.fori_loop(0, number, body, 0)


def copies(axis, extent, buf, send, recv):
    me = lax.axis_index(axis)
    started = []
    for k in range(1, extent):
        started.append(
            pltpu.make_async_remote_copy(
                src_ref=buf.at[me],
                dst_ref=buf.at[me],
                send_sem=send.at[k - 1],
                recv_sem=recv.at[k - 1],
                device_id={axis: lax.rem(me + k, extent)},
                device_id_type=MESH,
            )
        )
    return started


def arrival(axis, extent, buf, send, recv, k):
    me = lax.axis_index(axis)
    origin = lax.rem(me + extent - k, extent)
    return pltpu.make_async_remote_copy(
        src_ref=buf.at[origin],
        dst_ref=buf.at[origin],
        send_sem=send.at[k - 1],
        recv_sem=recv.at[k - 1],
        device_id={axis: origin},
        device_id_type=MESH,
    )


def exchange(axis, extent, buf, send, recv):
    started = copies(axis, extent, buf, send, recv)
    for copy in started:
        copy.start()
    for k in range(1, extent):
        arrival(axis, extent, buf, send, recv, k).wait_recv()
    return started


def merge(parts):
    top = jnp.max(parts, axis=0)
    return top + soft(jnp.sum(jnp.exp2((parts - top[None]) * SCALE), axis=0))


def kernel(
    nb, nc, feats, feats_pad,
    sc_ref, tc_ref, sm_ref, tm_ref,
    sp_ref, tp_ref, db_ref,
    blocks, a_right, a_left, b_right, b_left, rows, cols, lows, sums,
    g_send, g_recv, r_send, r_recv, c_send, c_recv, m_send, m_recv, d_send, d_recv,
):
    bi = lax.axis_index("blk")
    ci = lax.axis_index("col")
    ns = sc_ref.shape[1]
    ts = tc_ref.shape[1]
    gs = ns // LANES
    gt = ts // LANES
    barrier = pltpu.get_barrier_semaphore()
    for k in range(1, nb):
        pl.semaphore_signal(barrier, inc=1, device_id={"blk": lax.rem(bi + k, nb)}, device_id_type=MESH)
    for k in range(1, nc):
        pl.semaphore_signal(barrier, inc=1, device_id={"col": lax.rem(ci + k, nc)}, device_id_type=MESH)

    own = tc_ref[...].astype(F32)
    blocks[bi, 0:feats, :] = own
    for g in range(gt):
        lanes = slice(g * LANES, (g + 1) * LANES)
        blocks[bi, feats : feats + EXTRA, lanes] = row_tile(
            [tm_ref[g : g + 1, :], jnp.sum(jnp.square(own[:, lanes]), axis=0, keepdims=True)], LANES
        )

    depth = a_right.shape[0]
    ones = lambda width: jnp.where(
        lax.broadcasted_iota(jnp.int32, (depth - feats_pad, width), 0) < 3, 1.0, 0.0
    ).astype(BF16)

    pl.semaphore_wait(barrier, nb + nc - 2)
    gathers = copies("blk", nb, blocks, g_send, g_recv)
    for copy in gathers:
        copy.start()

    a_right[0:feats, :] = sc_ref[...]
    if feats_pad > feats:
        a_right[feats:feats_pad, :] = jnp.zeros((feats_pad - feats, ns), BF16)
        b_right[feats:feats_pad, :] = jnp.zeros((feats_pad - feats, b_right.shape[1]), BF16)
    a_right[feats_pad:depth, :] = ones(ns)
    b_right[feats_pad:depth, :] = ones(b_right.shape[1])
    wide = sc_ref[...].astype(F32)
    source_sq = jnp.sum(jnp.square(wide), axis=0, keepdims=True)
    for r in range(gs):
        rows_of = slice(r * LANES, (r + 1) * LANES)
        piece = jnp.concatenate(
            [wide[:, rows_of], jnp.zeros((feats_pad - feats, LANES), F32)], axis=0
        )
        a_left[rows_of, 0:feats_pad] = piece.T.astype(BF16)
    a_left[:, feats_pad:depth] = jnp.zeros((ns, depth - feats_pad), BF16)
    b_left[:, feats_pad:depth] = jnp.zeros((b_left.shape[0], depth - feats_pad), BF16)
    source_bias = EPSILON * jnp.log(sm_ref[...])

    for k in range(1, nb):
        arrival("blk", nb, blocks, g_send, g_recv, k).wait_recv()
    masses = []
    squares = []
    for b in range(nb):
        for g in range(gt):
            lanes = slice(g * LANES, (g + 1) * LANES)
            rows_of = slice(b * ts + g * LANES, b * ts + (g + 1) * LANES)
            piece = 2.0 * blocks[b, 0:feats, lanes]
            b_right[0:feats, rows_of] = piece.astype(BF16)
            if feats_pad > feats:
                piece = jnp.concatenate(
                    [piece, jnp.zeros((feats_pad - feats, LANES), F32)], axis=0
                )
            b_left[rows_of, 0:feats_pad] = piece.T.astype(BF16)
            masses.append(blocks[b, feats : feats + 1, lanes])
            squares.append(blocks[b, feats + 1 : feats + 2, lanes])
    target_mass = jnp.concatenate(masses, axis=0)
    target_sq = jnp.concatenate(squares, axis=0)
    target_bias = EPSILON * jnp.log(target_mass)

    chunk = 256
    pending = list(gathers)
    held = -target_sq
    for round_index in range(ROUNDS):
        set_bias(b_left, held + target_bias, feats_pad)
        part = rows.at[round_index]
        reduce_pass(b_left, a_right, part, ci, False, chunk)
        pending += exchange("col", nc, part, r_send.at[round_index], r_recv.at[round_index])
        set_bias(a_left, source_bias - merge(part[...]), feats_pad)
        part = cols.at[round_index]
        reduce_pass(a_left, b_right, part, bi, False, chunk)
        pending += exchange("blk", nb, part, c_send.at[round_index], c_recv.at[round_index])
        held = -merge(part[...])

    set_bias(b_left, held, feats_pad)
    reduce_pass(b_left, a_right, lows, ci, True, chunk)
    potential = held + target_sq
    lows[ci, gs : gs + 8, :] = jnp.broadcast_to(
        jnp.sum(target_mass * potential, axis=0, keepdims=True), (8, LANES)
    )
    pending += exchange("col", nc, lows, m_send, m_recv)
    for r in range(gs):
        lanes = slice(r * LANES, (r + 1) * LANES)
        best = jnp.max(lows[:, r, :], axis=0, keepdims=True)
        sp_ref[r : r + 1, :] = source_sq[:, lanes] - best
    target_part = jnp.sum(lows[:, gs, :], axis=0, keepdims=True)
    source_part = jnp.sum(sm_ref[...] * sp_ref[...], axis=0, keepdims=True)
    sums[bi] = jnp.broadcast_to(source_part, (8, LANES))
    pending += exchange("blk", nb, sums, d_send, d_recv)
    whole = jnp.sum(sums[...], axis=0)[0:1, :] + target_part
    db_ref[...] = jnp.sum(whole, axis=1, keepdims=True)
    cols_of = lax.broadcasted_iota(jnp.int32, potential.shape, 0)
    for g in range(gt):
        tp_ref[g : g + 1, :] = jnp.sum(
            jnp.where(cols_of == bi * gt + g, potential, 0.0), axis=0, keepdims=True
        )
    for copy in pending:
        copy.wait_send()


def local(nb, nc, source_coords, target_coords, source_mass, target_mass):
    feats, ns = source_coords.shape
    ts = target_coords.shape[1]
    nh = nb * ts
    gs, gh = ns // LANES, nh // LANES
    feats_pad = -(-feats // LANES) * LANES
    depth = feats_pad + LANES
    vmem = pl.BlockSpec(memory_space=pltpu.VMEM)
    dma = pltpu.SemaphoreType.DMA
    outs = pl.pallas_call(
        functools.partial(kernel, nb, nc, feats, feats_pad),
        out_shape=(
            jax.ShapeDtypeStruct((gs, LANES), F32),
            jax.ShapeDtypeStruct((ts // LANES, LANES), F32),
            jax.ShapeDtypeStruct((1, 1), F32),
        ),
        in_specs=[vmem] * 4,
        out_specs=(vmem,) * 3,
        scratch_shapes=[
            pltpu.VMEM((nb, feats + EXTRA, ts), F32),
            pltpu.VMEM((depth, ns), BF16),
            pltpu.VMEM((ns, depth), BF16),
            pltpu.VMEM((depth, nh), BF16),
            pltpu.VMEM((nh, depth), BF16),
            pltpu.VMEM((ROUNDS, nc, gs, LANES), F32),
            pltpu.VMEM((ROUNDS, nb, gh, LANES), F32),
            pltpu.VMEM((nc, gs + 8, LANES), F32),
            pltpu.VMEM((nb, 8, LANES), F32),
            dma((nb - 1,)), dma((nb - 1,)),
            dma((ROUNDS, nc - 1)), dma((ROUNDS, nc - 1)),
            dma((ROUNDS, nb - 1)), dma((ROUNDS, nb - 1)),
            dma((nc - 1,)), dma((nc - 1,)),
            dma((nb - 1,)), dma((nb - 1,)),
        ],
        compiler_params=pltpu.CompilerParams(
            collective_id=0, has_side_effects=True, vmem_limit_bytes=56 * 1024 * 1024
        ),
        name="transport",
    )(
        source_coords,
        target_coords,
        source_mass.reshape(gs, LANES),
        target_mass.reshape(ts // LANES, LANES),
    )
    return outs[0].reshape(ns), outs[1].reshape(ts), outs[2].reshape(())


def solution(mesh):
    in_specs = (P(None, "blk"), P(None, ("blk", "col")), P("blk"), P(("blk", "col")))
    out_specs = (P("blk"), P(("blk", "col")), P())
    body = functools.partial(local, mesh.shape["blk"], mesh.shape["col"])
    return jax.shard_map(body, mesh=mesh, in_specs=in_specs, out_specs=out_specs, check_vma=False)
```

time: 210 us -> 54 us (0.26)
  blocking collectives: 182 us -> 0 us
  Pallas kernels: 0 us -> 49.6 us
  other arithmetic: 19.1 us -> 0 us
  matrix products: 2.19 us -> 0 us
    all_gather x12 -> x0, blocking collectives: 135 us -> none  [the longest x8 88.1 us: merged(): pieces = jax.tree.map(lambda part: lax.all_gather(part, axis), value)]
    pallas_call x0 -> x1, Pallas kernels: none -> 49.6 us  [local(): pl.pallas_call(functools.partial(kernel, nb, nc, feats, feats_pad), out_s...]
    psum x1 -> x0, blocking collectives: 38.1 us -> none  [local(): lax.psum((source_part, target_part), ('blk', 'col'))]
    pmin x1 -> x0, blocking collectives: 8.94 us -> none  [local(): source_potential = lax.pmin(lowest, 'col')]
    reduce_max x3 -> x0, other arithmetic: 8.72 us -> none  [reduce_axis(): maxima = jnp.max(scores, axis=along)]
    reduce_sum x8 -> x0, other arithmetic: 6.71 us -> none  [the longest x4 4.32 us: reduce_axis(): jnp.sum(jnp.exp(scores - jnp.expand_dims(maxima, along)), axis=along)]
    reduce_min x1 -> x0, other arithmetic: 2.53 us -> none  [lower(): return (jnp.minimum(partial_value, jnp.min(values, axis=1)), None)]
    dot_general x1 -> x0, matrix products: 2.19 us -> none  [inner_products(): lax.dot_general(left_coords, right_coords, (((0,), (0,)), ((), ())), pref...]
where the time goes in v1:
time: 54 us; the launch traced here: 53.8 us
  Pallas kernels  49.6 us (92%)
  between operations  2.4 us (4%)
  local copies, waits for them, and re-layouts  1.82 us (3%)
    pallas_call x1, Pallas kernels, local(): pl.pallas_call(functools.partial(kernel, nb, nc, feats, feats_pad), out_s...  49.6 us
    unnamed x6, local copies, waits for them, and re-layouts  1.82 us

profile of v1, /device:TPU:0, one launch (start us, length us, event | category | flops | bytes accessed | tf_op | source)
XLA Modules:
  0.0 53.8 jit_solution(7051580982048456322)
XLA Ops:
  0.6 49.6 %transport.1 = (f32[8,128]{1,0:T(8,128)}, f32[1,128]{1,0:T(1,128)}, f32[1,1]{1,0:T(1,128)}) custom-call(bf16[96,1024]{1,0:T(8,128)(2,1)} %sc_ref.1, bf16[96,128]{1,0:T(8,128)(2,1)} %tc_ref.1, f32[8,128]{1,0:T(8,128)} %bitcast.5, f32[1,128]{1,0:T(1,128)} %bitcast.7), custom_call_target="tpu_custom_call" | custom-call | tf_op jit(solution)/shard_map/transport/pallas_call | solution.py:234
  50.3 0.0 copy-start
  50.3 0.7 %copy-done = f32[8,128]{1,0:T(8,128)S(1)} copy-done((f32[8,128]{1,0:T(8,128)S(1)}, f32[8,128]{1,0:T(8,128)}, u32[]{:S(2)}) %copy-start) | copy-done | bytes 4120
  51.0 0.0 copy-start.1
  51.0 0.6 %copy.10 = f32[1024]{0:T(1024)} copy(f32[1024]{0:T(1024)S(1)} %bitcast.6) | data formatting | bytes 8192
  51.5 0.0 copy-done.1
  51.6 0.5 copy.11
Async XLA Ops:
  50.3 0.7 %copy-start = (f32[8,128]{1,0:T(8,128)S(1)}, f32[8,128]{1,0:T(8,128)}, u32[]{:S(2)}) copy-start(f32[8,128]{1,0:T(8,128)} %get-tuple-element.6) | copy-start | bytes 12292
  51.0 0.6 %copy-start.1 = (f32[1,128]{1,0:T(1,128)S(1)}, f32[1,128]{1,0:T(1,128)}, u32[]{:S(2)}) copy-start(f32[1,128]{1,0:T(1,128)} %get-tuple-element.7) | copy-start | bytes 1540

commit v2 on v1

--- a/solution.py
+++ b/solution.py
@@ -10,6 +10,8 @@
 ROUNDS = 2
 EPSILON = 0.05
 LANES = 128
+WAYS = 4
+UNROLLED = 4 * 1024
 EXTRA = 8
 F32 = jnp.float32
 BF16 = jnp.bfloat16
@@ -43,15 +45,29 @@
         left_ref[r * LANES : (r + 1) * LANES, feats_pad : feats_pad + 8] = tile.T.astype(BF16)
 
 
+def folded(values, join, ways):
+    count = values.shape[0]
+    step = 8
+    chains = [values[w * step : (w + 1) * step, :] for w in range(ways)]
+    for r in range(ways, count // step):
+        chains[r % ways] = join(chains[r % ways], values[r * step : (r + 1) * step, :])
+    while len(chains) > 1:
+        half = len(chains) // 2
+        chains = [join(chains[i], chains[i + half]) for i in range(half)]
+    return chains[0]
+
+
 def reduce_pass(left_ref, right_ref, out_ref, slot, hard, chunk):
     number = right_ref.shape[1] // chunk
+    unrolled = number * left_ref.shape[0] <= UNROLLED
 
     def body(c, carry):
-        lanes = pl.ds(pl.multiple_of(c * chunk, chunk), chunk)
+        lanes = pl.ds(c * chunk if unrolled else pl.multiple_of(c * chunk, chunk), chunk)
         scores = jnp.dot(left_ref[...], right_ref[:, lanes], preferred_element_type=F32)
-        value = jnp.max(scores, axis=0, keepdims=True)
+        value = jnp.max(folded(scores, jnp.maximum, WAYS), axis=0, keepdims=True)
         if not hard:
-            total = jnp.sum(jnp.exp2((scores - value) * SCALE), axis=0, keepdims=True)
+            terms = jnp.exp2((scores - value) * SCALE)
+            total = jnp.sum(folded(terms, jnp.add, WAYS), axis=0, keepdims=True)
             value = value + soft(total)
         for r in range(chunk // LANES):
             out_ref[slot, pl.ds(c * (chunk // LANES) + r, 1), :] = value[
@@ -59,7 +75,11 @@
             ]
         return carry
 
-    lax.fori_loop(0, number, body, 0)
+    if unrolled:
+        for c in range(number):
+            body(c, 0)
+    else:
+        lax.fori_loop(0, number, body, 0)
 
 
 def copies(axis, extent, buf, send, recv):
@@ -108,9 +128,9 @@
 
 def kernel(
     nb, nc, feats, feats_pad,
-    sc_ref, tc_ref, sm_ref, tm_ref,
+    sc_any, tc_any, sm_any, tm_any,
     sp_ref, tp_ref, db_ref,
-    blocks, a_right, a_left, b_right, b_left, rows, cols, lows, sums,
+    sc_ref, tc_ref, sm_ref, tm_ref, in_sem, f_send, f_recv, blocks, a_right, a_left, b_right, b_left, rows, cols, lows, sums,
     g_send, g_recv, r_send, r_recv, c_send, c_recv, m_send, m_recv, d_send, d_recv,
 ):
     bi = lax.axis_index("blk")
@@ -119,12 +139,22 @@
     ts = tc_ref.shape[1]
     gs = ns // LANES
     gt = ts // LANES
+    loads = [
+        pltpu.make_async_copy(src, dst, in_sem.at[index])
+        for index, (src, dst) in enumerate(
+            ((tc_any, tc_ref), (tm_any, tm_ref), (sc_any, sc_ref), (sm_any, sm_ref))
+        )
+    ]
+    for load in loads:
+        load.start()
     barrier = pltpu.get_barrier_semaphore()
     for k in range(1, nb):
         pl.semaphore_signal(barrier, inc=1, device_id={"blk": lax.rem(bi + k, nb)}, device_id_type=MESH)
     for k in range(1, nc):
         pl.semaphore_signal(barrier, inc=1, device_id={"col": lax.rem(ci + k, nc)}, device_id_type=MESH)
 
+    loads[0].wait()
+    loads[1].wait()
     own = tc_ref[...].astype(F32)
     blocks[bi, 0:feats, :] = own
     for g in range(gt):
@@ -138,10 +168,28 @@
         lax.broadcasted_iota(jnp.int32, (depth - feats_pad, width), 0) < 3, 1.0, 0.0
     ).astype(BF16)
 
+    half = nb // 2
+    sibling = bi + 1 - 2 * lax.rem(bi, 2)
+
+    def shipment(block, peer, send, recv):
+        return pltpu.make_async_remote_copy(
+            src_ref=blocks.at[block],
+            dst_ref=blocks.at[block],
+            send_sem=send,
+            recv_sem=recv,
+            device_id={"blk": peer},
+            device_id_type=MESH,
+        )
+
     pl.semaphore_wait(barrier, nb + nc - 2)
-    gathers = copies("blk", nb, blocks, g_send, g_recv)
+    gathers = [
+        shipment(bi, lax.rem(bi + 2 * j, nb), g_send.at[j], g_recv.at[j]) for j in range(1, half)
+    ]
+    gathers.append(shipment(bi, sibling, g_send.at[0], g_recv.at[0]))
     for copy in gathers:
         copy.start()
+    loads[2].wait()
+    loads[3].wait()
 
     a_right[0:feats, :] = sc_ref[...]
     if feats_pad > feats:
@@ -161,14 +209,10 @@
     b_left[:, feats_pad:depth] = jnp.zeros((b_left.shape[0], depth - feats_pad), BF16)
     source_bias = EPSILON * jnp.log(sm_ref[...])
 
-    for k in range(1, nb):
-        arrival("blk", nb, blocks, g_send, g_recv, k).wait_recv()
-    masses = []
-    squares = []
-    for b in range(nb):
+    def unpack(b):
         for g in range(gt):
             lanes = slice(g * LANES, (g + 1) * LANES)
-            rows_of = slice(b * ts + g * LANES, b * ts + (g + 1) * LANES)
+            rows_of = pl.ds(pl.multiple_of(b * ts + g * LANES, LANES), LANES)
             piece = 2.0 * blocks[b, 0:feats, lanes]
             b_right[0:feats, rows_of] = piece.astype(BF16)
             if feats_pad > feats:
@@ -176,6 +220,27 @@
                     [piece, jnp.zeros((feats_pad - feats, LANES), F32)], axis=0
                 )
             b_left[rows_of, 0:feats_pad] = piece.T.astype(BF16)
+
+    unpack(bi)
+    shipment(sibling, sibling, g_send.at[0], g_recv.at[0]).wait_recv()
+    unpack(sibling)
+    order = [j // 2 + 1 if j % 2 == 0 else half - 1 - j // 2 for j in range(half - 1)]
+    for j in order:
+        origin = lax.rem(bi + nb - 2 * j, nb)
+        shipment(origin, origin, g_send.at[j], g_recv.at[j]).wait_recv()
+        forward = shipment(origin, sibling, f_send.at[j], f_recv.at[j])
+        forward.start()
+        gathers.append(forward)
+        unpack(origin)
+    for j in order:
+        origin = lax.rem(sibling + nb - 2 * j, nb)
+        shipment(origin, sibling, f_send.at[j], f_recv.at[j]).wait_recv()
+        unpack(origin)
+    masses = []
+    squares = []
+    for b in range(nb):
+        for g in range(gt):
+            lanes = slice(g * LANES, (g + 1) * LANES)
             masses.append(blocks[b, feats : feats + 1, lanes])
             squares.append(blocks[b, feats + 1 : feats + 2, lanes])
     target_mass = jnp.concatenate(masses, axis=0)
@@ -202,6 +267,11 @@
     lows[ci, gs : gs + 8, :] = jnp.broadcast_to(
         jnp.sum(target_mass * potential, axis=0, keepdims=True), (8, LANES)
     )
+    cols_of = lax.broadcasted_iota(jnp.int32, potential.shape, 0)
+    for g in range(gt):
+        tp_ref[g : g + 1, :] = jnp.sum(
+            jnp.where(cols_of == bi * gt + g, potential, 0.0), axis=0, keepdims=True
+        )
     pending += exchange("col", nc, lows, m_send, m_recv)
     for r in range(gs):
         lanes = slice(r * LANES, (r + 1) * LANES)
@@ -213,11 +283,6 @@
     pending += exchange("blk", nb, sums, d_send, d_recv)
     whole = jnp.sum(sums[...], axis=0)[0:1, :] + target_part
     db_ref[...] = jnp.sum(whole, axis=1, keepdims=True)
-    cols_of = lax.broadcasted_iota(jnp.int32, potential.shape, 0)
-    for g in range(gt):
-        tp_ref[g : g + 1, :] = jnp.sum(
-            jnp.where(cols_of == bi * gt + g, potential, 0.0), axis=0, keepdims=True
-        )
     for copy in pending:
         copy.wait_send()
 
@@ -238,9 +303,14 @@
             jax.ShapeDtypeStruct((ts // LANES, LANES), F32),
             jax.ShapeDtypeStruct((1, 1), F32),
         ),
-        in_specs=[vmem] * 4,
+        in_specs=[pl.BlockSpec(memory_space=pl.ANY)] * 4,
         out_specs=(vmem,) * 3,
         scratch_shapes=[
+            pltpu.VMEM((feats, ns), BF16),
+            pltpu.VMEM((feats, ts), BF16),
+            pltpu.VMEM((gs, LANES), F32),
+            pltpu.VMEM((ts // LANES, LANES), F32),
+            dma((4,)), dma((nb // 2,)), dma((nb // 2,)),
             pltpu.VMEM((nb, feats + EXTRA, ts), F32),
             pltpu.VMEM((depth, ns), BF16),
             pltpu.VMEM((ns, depth), BF16),
@@ -250,7 +320,7 @@
             pltpu.VMEM((ROUNDS, nb, gh, LANES), F32),
             pltpu.VMEM((nc, gs + 8, LANES), F32),
             pltpu.VMEM((nb, 8, LANES), F32),
-            dma((nb - 1,)), dma((nb - 1,)),
+            dma((nb // 2,)), dma((nb // 2,)),
             dma((ROUNDS, nc - 1)), dma((ROUNDS, nc - 1)),
             dma((ROUNDS, nb - 1)), dma((ROUNDS, nb - 1)),
             dma((nc - 1,)), dma((nc - 1,)),

time: 54 us -> 45.1 us (0.84)
  Pallas kernels: 49.6 us -> 40.7 us
    pallas_call x1, Pallas kernels: 49.6 us -> 40.7 us  [local(): pl.pallas_call(functools.partial(kernel, nb, nc, feats, feats_pad), out_s...]
where the time goes in v2:
time: 45.1 us; the launch traced here: 45 us
  Pallas kernels  40.7 us (90%)
  between operations  2.4 us (5%)
  local copies, waits for them, and re-layouts  1.82 us (4%)
    pallas_call x1, Pallas kernels, local(): pl.pallas_call(functools.partial(kernel, nb, nc, feats, feats_pad), out_s...  40.7 us
    unnamed x6, local copies, waits for them, and re-layouts  1.82 us

profile of v2, /device:TPU:0, one launch (start us, length us, event | category | flops | bytes accessed | tf_op | source)
XLA Modules:
  0.0 45.0 jit_solution(2164216825199151450)
XLA Ops:
  0.6 40.7 %transport.1 = (f32[8,128]{1,0:T(8,128)}, f32[1,128]{1,0:T(1,128)}, f32[1,1]{1,0:T(1,128)}) custom-call(bf16[96,1024]{1,0:T(8,128)(2,1)} %sc_any.1, bf16[96,128]{1,0:T(8,128)(2,1)} %tc_any.1, f32[8,128]{1,0:T(8,128)} %bitcast.5, f32[1,128]{1,0:T(1,128)} %bitcast.7), custom_call_target="tpu_custom_call" | custom-call | tf_op jit(solution)/shard_map/transport/pallas_call | solution.py:299
  41.4 0.0 copy-start
  41.4 0.7 %copy-done = f32[8,128]{1,0:T(8,128)S(1)} copy-done((f32[8,128]{1,0:T(8,128)S(1)}, f32[8,128]{1,0:T(8,128)}, u32[]{:S(2)}) %copy-start) | copy-done | bytes 4120
  42.1 0.0 copy-start.1
  42.1 0.6 %copy.10 = f32[1024]{0:T(1024)} copy(f32[1024]{0:T(1024)S(1)} %bitcast.6) | data formatting | bytes 8192
  42.7 0.0 copy-done.1
  42.7 0.5 %copy.11 = f32[128]{0:T(128)} copy(f32[128]{0:T(128)S(1)} %bitcast.8) | data formatting | bytes 1024
Async XLA Ops:
  41.4 0.7 %copy-start = (f32[8,128]{1,0:T(8,128)S(1)}, f32[8,128]{1,0:T(8,128)}, u32[]{:S(2)}) copy-start(f32[8,128]{1,0:T(8,128)} %get-tuple-element.6) | copy-start | bytes 12292
  42.1 0.6 %copy-start.1 = (f32[1,128]{1,0:T(1,128)S(1)}, f32[1,128]{1,0:T(1,128)}, u32[]{:S(2)}) copy-start(f32[1,128]{1,0:T(1,128)} %get-tuple-element.7) | copy-start | bytes 1540

commit v3 on v2

--- a/solution.py
+++ b/solution.py
@@ -10,7 +10,7 @@
 ROUNDS = 2
 EPSILON = 0.05
 LANES = 128
-WAYS = 4
+WAYS = 8
 UNROLLED = 4 * 1024
 EXTRA = 8
 F32 = jnp.float32
@@ -130,7 +130,7 @@
     nb, nc, feats, feats_pad,
     sc_any, tc_any, sm_any, tm_any,
     sp_ref, tp_ref, db_ref,
-    sc_ref, tc_ref, sm_ref, tm_ref, in_sem, f_send, f_recv, blocks, a_right, a_left, b_right, b_left, rows, cols, lows, sums,
+    sc_ref, tc_ref, sm_ref, tm_ref, in_sem, f_send, f_recv, firsts, blocks, a_right, a_left, b_right, b_left, rows, cols, lows, sums,
     g_send, g_recv, r_send, r_recv, c_send, c_recv, m_send, m_recv, d_send, d_recv,
 ):
     bi = lax.axis_index("blk")
@@ -199,13 +199,6 @@
     b_right[feats_pad:depth, :] = ones(b_right.shape[1])
     wide = sc_ref[...].astype(F32)
     source_sq = jnp.sum(jnp.square(wide), axis=0, keepdims=True)
-    for r in range(gs):
-        rows_of = slice(r * LANES, (r + 1) * LANES)
-        piece = jnp.concatenate(
-            [wide[:, rows_of], jnp.zeros((feats_pad - feats, LANES), F32)], axis=0
-        )
-        a_left[rows_of, 0:feats_pad] = piece.T.astype(BF16)
-    a_left[:, feats_pad:depth] = jnp.zeros((ns, depth - feats_pad), BF16)
     b_left[:, feats_pad:depth] = jnp.zeros((b_left.shape[0], depth - feats_pad), BF16)
     source_bias = EPSILON * jnp.log(sm_ref[...])
 
@@ -220,22 +213,46 @@
                     [piece, jnp.zeros((feats_pad - feats, LANES), F32)], axis=0
                 )
             b_left[rows_of, 0:feats_pad] = piece.T.astype(BF16)
+            bias = EPSILON * jnp.log(blocks[b, feats : feats + 1, lanes])
+            set_bias(
+                b_left.at[rows_of, :], bias - blocks[b, feats + 1 : feats + 2, lanes], feats_pad
+            )
 
     unpack(bi)
+    for r in range(gs):
+        rows_of = slice(r * LANES, (r + 1) * LANES)
+        piece = jnp.concatenate(
+            [wide[:, rows_of], jnp.zeros((feats_pad - feats, LANES), F32)], axis=0
+        )
+        a_left[rows_of, 0:feats_pad] = piece.T.astype(BF16)
+    a_left[:, feats_pad:depth] = jnp.zeros((ns, depth - feats_pad), BF16)
     shipment(sibling, sibling, g_send.at[0], g_recv.at[0]).wait_recv()
     unpack(sibling)
     order = [j // 2 + 1 if j % 2 == 0 else half - 1 - j // 2 for j in range(half - 1)]
-    for j in order:
+    def relay(j):
         origin = lax.rem(bi + nb - 2 * j, nb)
         shipment(origin, origin, g_send.at[j], g_recv.at[j]).wait_recv()
         forward = shipment(origin, sibling, f_send.at[j], f_recv.at[j])
         forward.start()
         gathers.append(forward)
-        unpack(origin)
-    for j in order:
+        return origin
+
+    def relayed(j):
         origin = lax.rem(sibling + nb - 2 * j, nb)
         shipment(origin, sibling, f_send.at[j], f_recv.at[j]).wait_recv()
         unpack(origin)
+
+    for index, j in enumerate(order):
+        if index >= 2:
+            relayed(order[index - 2])
+        origin = relay(j)
+        if index + 1 < len(order):
+            unpack(origin)
+        else:
+            if index >= 1:
+                relayed(order[index - 1])
+            unpack(origin)
+            relayed(j)
     masses = []
     squares = []
     for b in range(nb):
@@ -249,11 +266,14 @@
 
     chunk = 256
     pending = list(gathers)
-    held = -target_sq
+    held = None
     for round_index in range(ROUNDS):
-        set_bias(b_left, held + target_bias, feats_pad)
         part = rows.at[round_index]
-        reduce_pass(b_left, a_right, part, ci, False, chunk)
+        if round_index == 0:
+            reduce_pass(b_left, a_right, part, ci, False, chunk)
+        else:
+            set_bias(b_left, held + target_bias, feats_pad)
+            reduce_pass(b_left, a_right, part, ci, False, chunk)
         pending += exchange("col", nc, part, r_send.at[round_index], r_recv.at[round_index])
         set_bias(a_left, source_bias - merge(part[...]), feats_pad)
         part = cols.at[round_index]
@@ -311,6 +331,7 @@
             pltpu.VMEM((gs, LANES), F32),
             pltpu.VMEM((ts // LANES, LANES), F32),
             dma((4,)), dma((nb // 2,)), dma((nb // 2,)),
+            pltpu.VMEM((nb, gs, LANES), F32),
             pltpu.VMEM((nb, feats + EXTRA, ts), F32),
             pltpu.VMEM((depth, ns), BF16),
             pltpu.VMEM((ns, depth), BF16),

time: 45.1 us -> 45 us (level)
  no operation moved by 1% of the time
where the time goes in v3:
time: 45 us; the launch traced here: 44.8 us
  Pallas kernels  40.6 us (90%)
  between operations  2.4 us (5%)
  local copies, waits for them, and re-layouts  1.82 us (4%)
    pallas_call x1, Pallas kernels, local(): pl.pallas_call(functools.partial(kernel, nb, nc, feats, feats_pad), out_s...  40.6 us
    unnamed x6, local copies, waits for them, and re-layouts  1.82 us

profile of v3, /device:TPU:0, one launch (start us, length us, event | category | flops | bytes accessed | tf_op | source)
XLA Modules:
  0.0 44.8 jit_solution(10570584358878240264)
XLA Ops:
  0.6 40.6 %transport.1 = (f32[8,128]{1,0:T(8,128)}, f32[1,128]{1,0:T(1,128)}, f32[1,1]{1,0:T(1,128)}) custom-call(bf16[96,1024]{1,0:T(8,128)(2,1)} %sc_any.1, bf16[96,128]{1,0:T(8,128)(2,1)} %tc_any.1, f32[8,128]{1,0:T(8,128)} %bitcast.5, f32[1,128]{1,0:T(1,128)} %bitcast.7), custom_call_target="tpu_custom_call" | custom-call | tf_op jit(solution)/shard_map/transport/pallas_call | solution.py:319
  41.3 0.0 copy-start
  41.3 0.7 %copy-done = f32[8,128]{1,0:T(8,128)S(1)} copy-done((f32[8,128]{1,0:T(8,128)S(1)}, f32[8,128]{1,0:T(8,128)}, u32[]{:S(2)}) %copy-start) | copy-done | bytes 4120
  42.0 0.0 copy-start.1
  42.0 0.6 %copy.10 = f32[1024]{0:T(1024)} copy(f32[1024]{0:T(1024)S(1)} %bitcast.6) | data formatting | bytes 8192
  42.5 0.0 copy-done.1
  42.6 0.5 %copy.11 = f32[128]{0:T(128)} copy(f32[128]{0:T(128)S(1)} %bitcast.8) | data formatting | bytes 1024
Async XLA Ops:
  41.3 0.7 %copy-start = (f32[8,128]{1,0:T(8,128)S(1)}, f32[8,128]{1,0:T(8,128)}, u32[]{:S(2)}) copy-start(f32[8,128]{1,0:T(8,128)} %get-tuple-element.6) | copy-start | bytes 12292
  42.0 0.6 %copy-start.1 = (f32[1,128]{1,0:T(1,128)S(1)}, f32[1,128]{1,0:T(1,128)}, u32[]{:S(2)}) copy-start(f32[1,128]{1,0:T(1,128)} %get-tuple-element.7) | copy-start | bytes 1540
